TPU v7x, 512 devices: a whole 4x8x8 slice. The times are simulated.
512 devices in a mesh: leaf: 8 (over z), row: 4 (over x), col: 16 (over y, core).
Axes of the slice: x: 4, y: 8, z: 8, core: 2. Of those that a mesh axis runs over, the one named last changes fastest.
Arguments:
- leaf_rhs: float32 [16, 16, 4096], P('leaf', None, 'col'), may hold values from -6 to 6
- leaf_inverse: float32 [16, 4096, 4096], P('leaf', 'row', 'col'), as said below
- update_rows: float32 [16, 2048, 4096], P('leaf', 'col', 'row'), may hold values from -0.09375 to 0.09375
- update_map: int32 [16, 16], P('leaf'), may hold values from 0 to 31, as said below
- sep_rhs: float32 [16, 4096], replicated, may hold values from -6 to 6
- sep_inverse: float32 [4096, 4096], P(('leaf', 'row', 'col')), as said below
Outputs:
- leaf_solution: float32 [16, 16, 4096], P('leaf', None, ('col', 'row'))
- sep_solution: float32 [16, 4096], P(None, ('leaf', 'row', 'col'))
Inputs may be any that keep to these rules, and one draw needn't show every extreme that they name: `update_map`: each row names 16 different separator blocks. `leaf_inverse`: entries off the diagonal are independent and of order 1 / sqrt(4096); each diagonal entry is one plus such a term. `sep_inverse`: entries off the diagonal are independent and of order 1 / sqrt(4096); each diagonal entry is one plus such a term.
All inputs are finite; a program needn't handle non-finite values.
Results may differ from a plain program's by a relative error of at most 0.000068.
Values sent between devices are 32-bit elements; how exact they have to be, the bound alone decides.
A program may use at most 64 MiB of HBM per device.

v0:
```python
import jax
import jax.numpy as jnp
from jax import lax
from jax.sharding import PartitionSpec as P

BLOCK = 128
HIGH = lax.Precision.HIGHEST


def body(leaf_rhs, leaf_inverse, update_rows, update_map, sep_rhs, sep_inverse):
    subs = leaf_rhs.shape[0]
    nrhs = leaf_rhs.shape[1]
    width = sep_rhs.shape[1]
    blocks_total = width // BLOCK
    blocks_here = update_rows.shape[1] // BLOCK
    first_block = lax.axis_index("col") * blocks_here
    local_map = lax.dynamic_slice_in_dim(update_map, first_block, blocks_here, 1)
    onehot = (
        local_map[:, :, None] == jnp.arange(blocks_total, dtype=jnp.int32)[None, None, :]
    ).astype(jnp.float32)
    partial_fwd = jnp.einsum("sij,srj->sri", leaf_inverse, leaf_rhs, precision=HIGH)
    forward = lax.psum(partial_fwd, "col")
    coupled = jnp.einsum("sun,srn->sru", update_rows, forward, precision=HIGH)
    coupled = coupled.reshape(subs, nrhs, blocks_here, BLOCK)
    contrib = jnp.einsum("srkc,skb->rbc", coupled, onehot, precision=HIGH).reshape(nrhs, width)
    sep_rows = sep_inverse.shape[0]
    row_start = lax.axis_index(("leaf", "row", "col")) * sep_rows
    total = lax.psum(contrib, ("leaf", "row", "col"))
    updated = sep_rhs - total
    sep_forward = jnp.einsum("ij,rj->ri", sep_inverse, updated, precision=HIGH)
    back_terms = jnp.einsum("ij,ri->rj", sep_inverse, sep_forward, precision=HIGH)
    sep_whole = lax.psum(back_terms, ("leaf", "row", "col"))
    sep_solution = lax.dynamic_slice_in_dim(sep_whole, row_start, sep_rows, 1)
    pulled = jnp.einsum(
        "rbc,skb->srkc", sep_whole.reshape(nrhs, blocks_total, BLOCK), onehot, precision=HIGH
    )
    pulled = pulled.reshape(subs, nrhs, blocks_here * BLOCK)
    pull_terms = jnp.einsum("sun,sru->srn", update_rows, pulled, precision=HIGH)
    pull_total = lax.psum(pull_terms, "col")
    reduced = forward - pull_total
    column_terms = jnp.einsum("sij,sri->srj", leaf_inverse, reduced, precision=HIGH)
    leaf_solution = lax.psum_scatter(column_terms, "row", scatter_dimension=2, tiled=True)
    return (leaf_solution, sep_solution)


def solution(mesh):
    in_specs = (
        P("leaf", None, "col"),
        P("leaf", "row", "col"),
        P("leaf", "col", "row"),
        P("leaf", None),
        P(),
        P(("leaf", "row", "col"), None),
    )
    out_specs = (P("leaf", None, ("col", "row")), P(None, ("leaf", "row", "col")))
    return jax.shard_map(body, mesh=mesh, in_specs=in_specs, out_specs=out_specs, check_vma=False)
```

profile of v0, /device:TPU:8, one launch (start us, length us, event | category | flops | bytes accessed | tf_op | source)
XLA Modules:
  0.0 833.5 jit_solution(7228872072157452738)
XLA Ops:
  7.2 0.0 copy-start
  7.2 0.0 copy-start.4
  7.2 0.0 copy-start.1
  7.2 0.0 copy-start.3
  7.2 0.0 all-reduce.5.cloned.1.call-start
  7.3 1.5 copy-done
  8.8 3.2 fusion.17
  12.0 0.0 all-reduce.5.cloned.1.call-update
  12.0 0.0 all-reduce.7.cloned.1.call-start
  12.1 0.0 copy-done.4
  12.1 0.2 dynamic-slice_reduce_fusion
  12.3 117.6 %all-reduce.5.cloned.1.call-done = f32[2,16,1024]{2,1,0:T(8,128)} async-done(((f32[2,16,1024]{2,1,0:T(8,128)}), f32[2,16,1024]{2,1,0:T(8,128)}) %all-reduce.5.cloned.1.call-update) | async-done | bytes 131088 | tf_op jit(solution)/shard_map/psum | solution.py:22
  129.9 0.0 copy-done.1
  129.9 1.9 fusion.18
  131.8 0.4 fusion.6
  132.2 0.0 copy-start.2
  132.2 0.9 copy.21
  133.1 0.0 all-reduce.7.cloned.1.call-update
  133.1 0.0 all-reduce.9.cloned.1.call-start
  133.2 275.3 %all-reduce.7.cloned.1.call-done = f32[16,4096]{1,0:T(8,128)} async-done(((f32[16,4096]{1,0:T(8,128)}), f32[16,4096]{1,0:T(8,128)}) %all-reduce.7.cloned.1.call-update) | async-done | bytes 262160 | tf_op jit(solution)/shard_map/psum | solution.py:28
  408.4 0.0 copy-done.3
  408.4 1.5 fusion
  409.9 1.1 fusion.19
  411.0 0.0 all-reduce.9.cloned.1.call-update
  411.0 0.0 all-reduce.11.cloned.1.call-start
  411.1 270.1 %all-reduce.9.cloned.1.call-done = f32[16,4096]{1,0:T(8,128)} async-done(((f32[16,4096]{1,0:T(8,128)}), f32[16,4096]{1,0:T(8,128)}) %all-reduce.9.cloned.1.call-update) | async-done | bytes 262160 | tf_op jit(solution)/shard_map/psum | solution.py:32
  681.1 1.0 copy.15
  682.1 0.2 fusion.8
  682.4 1.3 fusion.4
  683.6 0.0 all-reduce.11.cloned.1.call-update
  683.7 0.0 reduce-scatter.4.cloned.1.call-start
  683.7 110.0 %all-reduce.11.cloned.1.call-done = f32[2,16,1024]{2,1,0:T(8,128)} async-done(((f32[2,16,1024]{2,1,0:T(8,128)}), f32[2,16,1024]{2,1,0:T(8,128)}) %all-reduce.11.cloned.1.call-update) | async-done | bytes 131088 | tf_op jit(solution)/shard_map/psum | solution.py:39
  793.7 0.0 copy-done.2
  793.7 2.0 fusion.2
  795.7 0.1 copy.12
  795.9 0.9 reshape.76
  796.7 0.0 reduce-scatter.4.cloned.1.call-update
  796.8 0.8 constant_dynamic-slice_fusion
  797.6 0.7 copy.9
  798.2 27.2 %reduce-scatter.4.cloned.1.call-done = f32[64,32]{1,0:T(8,128)} async-done(((f32[256,32]{1,0:T(8,128)}), f32[64,32]{1,0:T(8,128)}) %reduce-scatter.4.cloned.1.call-update) | async-done | bytes 8208
  825.4 0.9 reshape.77
  826.3 0.7 copy.13
Async XLA Ops:
  7.2 1.6 copy-start
  7.2 4.9 copy-start.4
  7.2 122.7 %copy-start.1 = (f32[2,128,1024]{2,1,0:T(8,128)S(1)}, f32[2,128,1024]{2,1,0:T(8,128)}, u32[]{:S(2)}) copy-start(f32[2,128,1024]{2,1,0:T(8,128)} %param.8) | copy-start | bytes 3145732
  7.2 401.2 %copy-start.3 = (f32[8,4096]{1,0:T(8,128)S(1)}, f32[8,4096]{1,0:T(8,128)}, u32[]{:S(2)}) copy-start(f32[8,4096]{1,0:T(8,128)} %param.11) | copy-start | bytes 393220
  7.2 122.7 %all-reduce.5.cloned.1.call-start = ((), (), s32[]{:S(2)}) async-start(), calls=%async_computation.1 | async-start | bytes 262144 | tf_op jit(solution)/shard_map/psum | solution.py:22
  12.0 396.4 %all-reduce.7.cloned.1.call-start = ((), (), s32[]{:S(2)}) async-start(), calls=%async_computation.2 | async-start | bytes 524288 | tf_op jit(solution)/shard_map/psum | solution.py:28
  132.2 661.5 %copy-start.2 = (f32[2,16,1024]{2,1,0:T(8,128)S(1)}, f32[2,16,1024]{2,1,0:T(8,128)}, u32[]{:S(2)}) copy-start(f32[2,16,1024]{2,1,0:T(8,128)} %all-reduce.5.cloned.1.call-done) | copy-start | bytes 393220
  133.1 548.0 %all-reduce.9.cloned.1.call-start = ((), (), s32[]{:S(2)}) async-start(), calls=%async_computation.3 | async-start | bytes 524288 | tf_op jit(solution)/shard_map/psum | solution.py:32
  411.0 382.7 %all-reduce.11.cloned.1.call-start = ((), (), s32[]{:S(2)}) async-start(), calls=%async_computation.4 | async-start | bytes 262144 | tf_op jit(solution)/shard_map/psum | solution.py:39
  683.7 141.8 %reduce-scatter.4.cloned.1.call-start = ((), (), s32[]{:S(2)}) async-start(), calls=%async_computation.5 | async-start | bytes 163840
Sparse Core Ops, SparseCore 0:
  12.1 117.7 all-reduce.4
  134.9 273.4 all-reduce.6
  413.4 267.6 all-reduce.8
  683.8 109.8 all-reduce.10
  796.9 28.5 reduce-scatter.3
where the time goes:
time: 834 us
  waiting for transfers between devices  800 us (96%)
  between operations  13.9 us (2%)
  matrix products  11.6 us (1%)
    psum x1, waiting for transfers between devices, body(): total = lax.psum(contrib, ('leaf', 'row', 'col'))  275 us
    psum x1, waiting for transfers between devices, body(): sep_whole = lax.psum(back_terms, ('leaf', 'row', 'col'))  270 us
    psum x1, waiting for transfers between devices, body(): forward = lax.psum(partial_fwd, 'col')  118 us
    psum x1, waiting for transfers between devices, body(): pull_total = lax.psum(pull_terms, 'col')  110 us
    unnamed x6, waiting for transfers between devices  27.3 us
  transfers between devices with their start and end apart: 5, of which 5 were waited for; matrix products, arithmetic and copies ran while one was open for 0% of the time, Pallas kernels for 0%

commit v1 on v0

--- a/solution.py
+++ b/solution.py
@@ -29,7 +29,7 @@
     updated = sep_rhs - total
     sep_forward = jnp.einsum("ij,rj->ri", sep_inverse, updated, precision=HIGH)
     back_terms = jnp.einsum("ij,ri->rj", sep_inverse, sep_forward, precision=HIGH)
-    sep_whole = lax.psum(back_terms, ("leaf", "row", "col"))
+    sep_whole = lax.psum(lax.psum(back_terms, ("row", "col")), "leaf")
     sep_solution = lax.dynamic_slice_in_dim(sep_whole, row_start, sep_rows, 1)
     pulled = jnp.einsum(
         "rbc,skb->srkc", sep_whole.reshape(nrhs, blocks_total, BLOCK), onehot, precision=HIGH

time: 834 us -> 831 us (level)
    psum x1 -> x2, waiting for transfers between devices: 270 us -> 265 us  [body(): sep_whole = lax.psum(lax.psum(back_terms, ('row', 'col')), 'leaf')]
    unnamed x6 -> x7, waiting for transfers between devices: 27.3 us -> 27.3 us
  transfers between devices with their start and end apart: 5 -> 6, of which waited for: 5 -> 6; matrix products, arithmetic and copies ran while one was open for 0% -> 0% of each run, Pallas kernels for 0% -> 0%
where the time goes in v1:
time: 831 us; the launch traced here: 830 us
  waiting for transfers between devices  797 us (96%)
  between operations  14.2 us (2%)
  matrix products  11.6 us (1%)
    psum x1, waiting for transfers between devices, body(): total = lax.psum(contrib, ('leaf', 'row', 'col'))  275 us
    psum x2, waiting for transfers between devices, body(): sep_whole = lax.psum(lax.psum(back_terms, ('row', 'col')), 'leaf')  265 us
    psum x1, waiting for transfers between devices, body(): forward = lax.psum(partial_fwd, 'col')  118 us
    psum x1, waiting for transfers between devices, body(): pull_total = lax.psum(pull_terms, 'col')  111 us
    unnamed x7, waiting for transfers between devices  27.3 us
  transfers between devices with their start and end apart: 6, of which 6 were waited for; matrix products, arithmetic and copies ran while one was open for 0% of the time, Pallas kernels for 0%

profile of v1, /device:TPU:8, one launch (start us, length us, event | category | flops | bytes accessed | tf_op | source)
XLA Modules:
  0.0 830.4 jit_solution(17563032056601868439)
XLA Ops:
  7.2 0.0 copy-start
  7.2 0.0 copy-start.4
  7.2 0.0 copy-start.1
  7.2 0.0 copy-start.3
  7.2 0.0 all-reduce.6.cloned.1.call-start
  7.3 1.5 copy-done
  8.8 3.2 fusion.17
  12.0 0.0 all-reduce.6.cloned.1.call-update
  12.0 0.0 all-reduce.8.cloned.1.call-start
  12.1 0.0 copy-done.4
  12.1 0.2 dynamic-slice_reduce_fusion
  12.3 117.6 %all-reduce.6.cloned.1.call-done = f32[2,16,1024]{2,1,0:T(8,128)} async-done(((f32[2,16,1024]{2,1,0:T(8,128)}), f32[2,16,1024]{2,1,0:T(8,128)}) %all-reduce.6.cloned.1.call-update) | async-done | bytes 131088 | tf_op jit(solution)/shard_map/psum | solution.py:22
  129.9 0.0 copy-done.1
  129.9 1.9 fusion.18
  131.8 0.4 fusion.6
  132.2 0.9 copy.21
  133.1 0.0 copy-start.2
  133.1 0.0 all-reduce.8.cloned.1.call-update
  133.1 0.0 all-reduce.10.cloned.1.call-start
  133.1 275.3 %all-reduce.8.cloned.1.call-done = f32[16,4096]{1,0:T(8,128)} async-done(((f32[16,4096]{1,0:T(8,128)}), f32[16,4096]{1,0:T(8,128)}) %all-reduce.8.cloned.1.call-update) | async-done | bytes 262160 | tf_op jit(solution)/shard_map/psum | solution.py:28
  408.4 0.0 copy-done.3
  408.4 1.5 fusion
  409.9 1.1 fusion.19
  411.0 0.0 all-reduce.10.cloned.1.call-update
  411.0 0.0 all-reduce.12.cloned.1.call-start
  411.0 184.7 %all-reduce.10.cloned.1.call-done = f32[16,4096]{1,0:T(8,128)} async-done(((f32[16,4096]{1,0:T(8,128)}), f32[16,4096]{1,0:T(8,128)}) %all-reduce.10.cloned.1.call-update) | async-done | bytes 262160 | tf_op jit(solution)/shard_map/psum | solution.py:32
  595.8 0.0 all-reduce.12.cloned.1.call-update
  595.8 0.0 all-reduce.14.cloned.1.call-start
  595.8 80.5 %all-reduce.12.cloned.1.call-done = f32[16,4096]{1,0:T(8,128)} async-done(((f32[16,4096]{1,0:T(8,128)}), f32[16,4096]{1,0:T(8,128)}) %all-reduce.12.cloned.1.call-update) | async-done | bytes 262160 | tf_op jit(solution)/shard_map/psum | solution.py:32
  676.4 1.0 copy.15
  677.4 0.2 fusion.8
  677.6 1.3 fusion.4
  678.9 0.0 all-reduce.14.cloned.1.call-update
  678.9 0.0 reduce-scatter.4.cloned.1.call-start
  679.0 111.4 %all-reduce.14.cloned.1.call-done = f32[2,16,1024]{2,1,0:T(8,128)} async-done(((f32[2,16,1024]{2,1,0:T(8,128)}), f32[2,16,1024]{2,1,0:T(8,128)}) %all-reduce.14.cloned.1.call-update) | async-done | bytes 131088 | tf_op jit(solution)/shard_map/psum | solution.py:39
  790.3 0.0 copy-done.2
  790.3 2.0 fusion.2
  792.3 0.1 copy.12
  792.5 0.9 reshape.76
  793.4 0.0 reduce-scatter.4.cloned.1.call-update
  793.4 0.8 constant_dynamic-slice_fusion
  794.2 0.7 copy.9
  794.8 27.2 %reduce-scatter.4.cloned.1.call-done = f32[64,32]{1,0:T(8,128)} async-done(((f32[256,32]{1,0:T(8,128)}), f32[64,32]{1,0:T(8,128)}) %reduce-scatter.4.cloned.1.call-update) | async-done | bytes 8208
  822.1 0.9 reshape.77
  822.9 0.7 copy.13
Async XLA Ops:
  7.2 1.6 copy-start
  7.2 4.9 copy-start.4
  7.2 122.7 %copy-start.1 = (f32[2,128,1024]{2,1,0:T(8,128)S(1)}, f32[2,128,1024]{2,1,0:T(8,128)}, u32[]{:S(2)}) copy-start(f32[2,128,1024]{2,1,0:T(8,128)} %param.8) | copy-start | bytes 3145732
  7.2 401.2 %copy-start.3 = (f32[8,4096]{1,0:T(8,128)S(1)}, f32[8,4096]{1,0:T(8,128)}, u32[]{:S(2)}) copy-start(f32[8,4096]{1,0:T(8,128)} %param.11) | copy-start | bytes 393220
  7.2 122.7 %all-reduce.6.cloned.1.call-start = ((), (), s32[]{:S(2)}) async-start(), calls=%async_computation.1 | async-start | bytes 262144 | tf_op jit(solution)/shard_map/psum | solution.py:22
  12.0 396.4 %all-reduce.8.cloned.1.call-start = ((), (), s32[]{:S(2)}) async-start(), calls=%async_computation.2 | async-start | bytes 524288 | tf_op jit(solution)/shard_map/psum | solution.py:28
  133.1 657.2 %copy-start.2 = (f32[2,16,1024]{2,1,0:T(8,128)S(1)}, f32[2,16,1024]{2,1,0:T(8,128)}, u32[]{:S(2)}) copy-start(f32[2,16,1024]{2,1,0:T(8,128)} %all-reduce.6.cloned.1.call-done) | copy-start | bytes 393220
  133.1 462.7 %all-reduce.10.cloned.1.call-start = ((), (), s32[]{:S(2)}) async-start(), calls=%async_computation.3 | async-start | bytes 524288 | tf_op jit(solution)/shard_map/psum | solution.py:32
  411.0 265.4 %all-reduce.12.cloned.1.call-start = ((), (), s32[]{:S(2)}) async-start(), calls=%async_computation.4 | async-start | bytes 524288 | tf_op jit(solution)/shard_map/psum | solution.py:32
  595.8 194.5 %all-reduce.14.cloned.1.call-start = ((), (), s32[]{:S(2)}) async-start(), calls=%async_computation.5 | async-start | bytes 262144 | tf_op jit(solution)/shard_map/psum | solution.py:39
  678.9 143.2 %reduce-scatter.4.cloned.1.call-start = ((), (), s32[]{:S(2)}) async-start(), calls=%async_computation.6 | async-start | bytes 163840
Sparse Core Ops, SparseCore 0:
  12.1 117.7 all-reduce.5
  134.9 273.4 all-reduce.7
  411.9 183.8 all-reduce.9
  597.9 78.3 all-reduce.11
  679.0 111.2 all-reduce.13
  793.5 28.5 reduce-scatter.3
